TPU v7x, 512 devices: a whole 4x8x8 slice. The times are simulated.
512 devices in a mesh: rows: 64 (over x, z, core), cols: 8 (over y).
Axes of the slice: x: 4, y: 8, z: 8, core: 2. Of those that a mesh axis runs over, the one named last changes fastest.
Arguments:
- right_sides: float32 [4, 64, 128, 256], P(None, 'rows'), may hold values from -6 to 6
- factor_blocks: bfloat16 [3, 64, 8, 8, 256, 256], P(None, 'rows', 'cols'), may hold values from -0.125 to 0.125
- diag_inverses: bfloat16 [4, 64, 256, 256], P(None, 'rows')
- source_ids: int32 [3, 64, 8, 8], P(None, 'rows', 'cols'), may hold values from 0 to 191, as said below
- block_counts: int32 [3, 64, 8], P(None, 'rows', 'cols'), may hold values from 1 to 8, as said below
Outputs:
- solution: float32 [4, 64, 128, 256], P(None, 'rows', 'cols')
Inputs may be any that keep to these rules, and one draw needn't show every extreme that they name: source_ids[l, t, c, k] = m * 64 + s names a supernode of a level m <= l with s % 8 == c. block_counts[l, t, c] slots of target t on group c hold blocks of the factor; slots at and past it are not part of the factor. In every level some target and group has all 8 slots live.
All inputs are finite; a program needn't handle non-finite values.
Results may differ from a plain program's by a relative error of at most 0.007.
Values may be sent and summed in bfloat16 or wider, within the bound.
A program may use at most 128 MiB of HBM per device.

v0:
```python
import jax
import jax.numpy as jnp
from jax import lax
from jax.sharding import PartitionSpec as P


def locate(source, row_count, col_count):
    return source // row_count * (row_count // col_count) + source % row_count // col_count


def slot_sum(running, blocks, chosen_ids, live_count, solved_store, row_count, col_count):

    def add_block(slot_index, partial_value):
        source = chosen_ids[slot_index]
        solved_piece = lax.dynamic_index_in_dim(
            solved_store, locate(source, row_count, col_count), 0, keepdims=False
        )
        factor_piece = lax.dynamic_index_in_dim(blocks, slot_index, 0, keepdims=False)
        return partial_value + jnp.dot(
            solved_piece, factor_piece, preferred_element_type=jnp.float32
        )

    return lax.fori_loop(0, live_count, add_block, running)


def shards(right_sides, factor_blocks, diag_inverses, source_ids, block_counts):
    row_count = lax.axis_size("rows")
    col_count = lax.axis_size("cols")
    level_count = right_sides.shape[0]
    rhs_count = right_sides.shape[2]
    block_width = right_sides.shape[3]
    share_rows = rhs_count // col_count
    col_index = lax.axis_index("cols")
    per_level = row_count // col_count
    solved_store = jnp.zeros(((level_count - 1) * per_level, rhs_count, block_width), jnp.bfloat16)
    partials = [jnp.zeros((rhs_count, block_width), jnp.float32)] * level_count
    solutions = []
    for level_index in range(level_count):
        if level_index > 0:
            partials[level_index] = slot_sum(
                partials[level_index],
                factor_blocks[level_index - 1, 0, 0],
                source_ids[level_index - 1, 0, 0],
                block_counts[level_index - 1, 0, 0],
                solved_store,
                row_count,
                col_count,
            )
        own_rhs = lax.dynamic_slice_in_dim(
            right_sides[level_index, 0], col_index * share_rows, share_rows, 0
        )
        if level_index > 0:
            own_rhs = own_rhs - lax.psum_scatter(
                partials[level_index], "cols", scatter_dimension=0, tiled=True
            )
        own_solution = jnp.dot(
            own_rhs.astype(jnp.bfloat16),
            diag_inverses[level_index, 0],
            preferred_element_type=jnp.float32,
        )
        solutions.append(own_solution)
        if level_index < level_count - 1:
            pieces = lax.all_gather(
                own_solution.astype(jnp.bfloat16)[None], "rows", axis=0, tiled=True
            )
            grouped = pieces.reshape(per_level, col_count, share_rows, block_width)
            regrouped = lax.all_to_all(grouped, "cols", split_axis=1, concat_axis=2, tiled=True)
            solved_store = solved_store.at[
                level_index * per_level : (level_index + 1) * per_level
            ].set(regrouped[:, 0])
    return jnp.stack(solutions)[:, None]


def solution(mesh):
    return jax.shard_map(
        shards,
        mesh=mesh,
        in_specs=(
            P(None, "rows", None, None),
            P(None, "rows", "cols", None, None, None),
            P(None, "rows", None, None),
            P(None, "rows", "cols", None),
            P(None, "rows", "cols"),
        ),
        out_specs=P(None, "rows", "cols", None),
        check_vma=False,
    )
```

profile of v0, /device:TPU:2, one launch (start us, length us, event | category | flops | bytes accessed | tf_op | source)
XLA Modules:
  0.0 462.0 jit_solution(18360709935676070336)
XLA Ops:
  6.5 0.9 slice.116
  7.5 1.0 fusion.40
  8.5 56.0 %all-gather = bf16[1024,256]{1,0:T(8,128)(2,1)S(1)} all-gather(bf16[16,256]{1,0:T(8,128)(2,1)S(1)} %get-tuple-element.425), channel_id=2, replica_groups=mesh['rows'=64,'cols'=8] {'rows'}, dimensions={0}, use_global_device_ids=true | all-gather | bytes 532480 | tf_op jit(solution)/shard_map/all_gather | solution.py:63
  64.5 0.8 copy.11
  65.4 7.1 %all-to-all-start = ((bf16[8,8,16,256]{3,2,0,1:T(8,128)(2,1)}), bf16[8,8,16,256]{3,2,0,1:T(8,128)(2,1)S(1)}, u32[]{:S(2)}, u32[]{:S(2)}) async-start(bf16[8,8,16,256]{3,2,0,1:T(8,128)(2,1)} %copy.11), calls=%async_computation | async-start | bytes 1048576 | tf_op jit(solution)/shard_map/all_to_all | solution.py:67
  73.7 3.5 slice_bitcast_fusion
  77.2 13.3 %all-to-all-done = bf16[8,8,16,256]{3,2,0,1:T(8,128)(2,1)S(1)} async-done(((bf16[8,8,16,256]{3,2,0,1:T(8,128)(2,1)}), bf16[8,8,16,256]{3,2,0,1:T(8,128)(2,1)S(1)}, u32[]{:S(2)}, u32[]{:S(2)}) %all-to-all-start) | async-done | bytes 524320 | tf_op jit(solution)/shard_map/all_to_all | solution.py:67
  90.7 21.3 %while.42 = (s32[]{:T(128)}, f32[128,256]{1,0:T(8,128)S(1)}, s32[]{:T(128)}, s32[8]{0:T(128)S(1)}, bf16[24,128,256]{2,1,0:T(8,128)(2,1)S(1)}, /*index=5*/bf16[8,...) while((s32[]{:T(128)}, f32[128,256]{1,0:T(8,128)S(1)}, ...), condition=%wide.region_1.2_spmd, body=%wide.region_0.0_spmd.sunk | while | flops 16810028 | bytes 459350 | solution.py:23
  94.8 1.1 convolution_add_fusion.6
  100.0 1.1 convolution_add_fusion.6
  101.7 0.7 dynamic_slice.141
  105.2 1.1 convolution_add_fusion.6
  110.3 1.1 convolution_add_fusion.6
  112.7 51.3 %reduce-scatter.4.cloned.1.call-done = f32[16,256]{1,0:T(8,128)} async-done(((f32[128,256]{1,0:T(8,128)}), f32[16,256]{1,0:T(8,128)}) %reduce-scatter.4.cloned.1.call-update) | async-done | bytes 16400 | tf_op jit(solution)/shard_map/reduce_scatter | solution.py:53
  164.0 1.1 fusion.41
  165.0 50.9 %all-gather.1 = bf16[1024,256]{1,0:T(8,128)(2,1)S(1)} all-gather(bf16[16,256]{1,0:T(8,128)(2,1)S(1)} %get-tuple-element.427), channel_id=3, replica_groups=mesh['rows'=64,'cols'=8] {'rows'}, dimensions={0}, use_global_device_ids=true | all-gather | bytes 532480 | tf_op jit(solution)/shard_map/all_gather | solution.py:63
  215.9 0.8 copy.13
  216.7 4.6 all-to-all-start.1
  221.4 18.0 %all-to-all-done.1 = bf16[8,8,16,256]{3,2,0,1:T(8,128)(2,1)S(1)} async-done(((bf16[8,8,16,256]{3,2,0,1:T(8,128)(2,1)}), bf16[8,8,16,256]{3,2,0,1:T(8,128)(2,1)S(1)}, u32[]{:S(2)}, u32[]{:S(2)}) %all-to-all-start.1) | async-done | bytes 524320 | tf_op jit(solution)/shard_map/all_to_all | solution.py:67
  239.4 15.6 %while.43 = (s32[]{:T(128)}, f32[128,256]{1,0:T(8,128)S(1)}, s32[]{:T(128)}, s32[8]{0:T(128)S(1)}, bf16[24,128,256]{2,1,0:T(8,128)(2,1)S(1)}, /*index=5*/bf16[8,...) while((s32[]{:T(128)}, f32[128,256]{1,0:T(8,128)S(1)}, ...), condition=%wide.region_4.5_spmd, body=%wide.region_3.4_spmd.sunk | while | flops 16810028 | bytes 459350 | solution.py:23
  243.3 1.1 convolution_add_fusion.7
  248.3 1.1 convolution_add_fusion.7
  253.3 1.1 convolution_add_fusion.7
  255.7 57.3 %reduce-scatter.6.cloned.1.call-done = f32[16,256]{1,0:T(8,128)} async-done(((f32[128,256]{1,0:T(8,128)}), f32[16,256]{1,0:T(8,128)}) %reduce-scatter.6.cloned.1.call-update) | async-done | bytes 16400 | tf_op jit(solution)/shard_map/reduce_scatter | solution.py:53
  313.1 1.1 fusion.42
  314.1 50.8 %all-gather.2 = bf16[1024,256]{1,0:T(8,128)(2,1)S(1)} all-gather(bf16[16,256]{1,0:T(8,128)(2,1)S(1)} %get-tuple-element.429), channel_id=4, replica_groups=mesh['rows'=64,'cols'=8] {'rows'}, dimensions={0}, use_global_device_ids=true | all-gather | bytes 532480 | tf_op jit(solution)/shard_map/all_gather | solution.py:63
  364.9 0.9 copy.15
  365.8 4.6 %all-to-all-start.2 = ((bf16[8,8,16,256]{3,2,0,1:T(8,128)(2,1)}), bf16[8,8,16,256]{3,2,0,1:T(8,128)(2,1)S(1)}, u32[]{:S(2)}, u32[]{:S(2)}) async-start(bf16[8,8,16,256]{3,2,0,1:T(8,128)(2,1)} %copy.15), calls=%async_computation.4 | async-start | bytes 1048576 | tf_op jit(solution)/shard_map/all_to_all | solution.py:67
  370.5 18.0 %all-to-all-done.2 = bf16[8,8,16,256]{3,2,0,1:T(8,128)(2,1)S(1)} async-done(((bf16[8,8,16,256]{3,2,0,1:T(8,128)(2,1)}), bf16[8,8,16,256]{3,2,0,1:T(8,128)(2,1)S(1)}, u32[]{:S(2)}, u32[]{:S(2)}) %all-to-all-start.2) | async-done | bytes 524320 | tf_op jit(solution)/shard_map/all_to_all | solution.py:67
  388.6 12.5 %while.44 = (s32[]{:T(128)}, f32[128,256]{1,0:T(8,128)S(1)}, s32[]{:T(128)}, s32[8]{0:T(128)S(1)}, bf16[24,128,256]{2,1,0:T(8,128)(2,1)S(1)}, /*index=5*/bf16[8,...) while((s32[]{:T(128)}, f32[128,256]{1,0:T(8,128)S(1)}, ...), condition=%wide.region_7.8_spmd, body=%wide.region_6.7_spmd.sunk | while | flops 16810028 | bytes 459350 | solution.py:23
  401.8 51.9 %reduce-scatter.8.cloned.1.call-done = f32[16,256]{1,0:T(8,128)} async-done(((f32[128,256]{1,0:T(8,128)}), f32[16,256]{1,0:T(8,128)}) %reduce-scatter.8.cloned.1.call-update) | async-done | bytes 16400 | tf_op jit(solution)/shard_map/reduce_scatter | solution.py:53
  453.7 1.1 convolution_bitcast_fusion
  (47 shorter events, 10.6 us)
Async XLA Ops:
  6.5 66.0 %copy-start.4 = (s32[3,1,1]{0,2,1:T(1,128)S(1)}, s32[3,1,1]{0,2,1:T(1,128)}, u32[]{:S(2)}) copy-start(s32[3,1,1]{0,2,1:T(1,128)} %param.21) | copy-start | bytes 40
  6.5 66.6 %copy-start.5 = (s32[3,1,1,8]{3,2,1,0:T(1,128)S(1)}, s32[3,1,1,8]{3,2,1,0:T(1,128)}, u32[]{:S(2)}) copy-start(s32[3,1,1,8]{3,2,1,0:T(1,128)} %param.20) | copy-start | bytes 292
  65.4 25.1 %all-to-all-start = ((bf16[8,8,16,256]{3,2,0,1:T(8,128)(2,1)}), bf16[8,8,16,256]{3,2,0,1:T(8,128)(2,1)S(1)}, u32[]{:S(2)}, u32[]{:S(2)}) async-start(bf16[8,8,16,256]{3,2,0,1:T(8,128)(2,1)} %copy.11), calls=%async_computation | async-start | bytes 1048576 | tf_op jit(solution)/shard_map/all_to_all | solution.py:67
  72.5 91.5 %reduce-scatter.4.cloned.1.call-start = ((), (), s32[]{:S(2)}) async-start(), calls=%async_computation.6 | async-start | bytes 147456 | tf_op jit(solution)/shard_map/reduce_scatter | solution.py:53
  90.7 22.0 %copy-start.3 = (f32[4,1,128,256]{3,2,1,0:T(8,128)S(1)}, f32[4,1,128,256]{3,2,1,0:T(8,128)}, u32[]{:S(2)}) copy-start(f32[4,1,128,256]{3,2,1,0:T(8,128)} %param.17) | copy-start | bytes 1572868
  112.0 0.7 copy-start.1
  216.7 22.7 %copy-start.7 = (s32[8]{0:T(128)S(1)}, s32[8]{0:T(128)}, u32[]{:S(2)}) copy-start(s32[8]{0:T(128)} %get-tuple-element.596) | copy-start | bytes 100
  216.7 22.6 %all-to-all-start.1 = ((bf16[8,8,16,256]{3,2,0,1:T(8,128)(2,1)}), bf16[8,8,16,256]{3,2,0,1:T(8,128)(2,1)S(1)}, u32[]{:S(2)}, u32[]{:S(2)}) async-start(bf16[8,8,16,256]{3,2,0,1:T(8,128)(2,1)} %copy.13), calls=%async_computation.2 | async-start | bytes 1048576 | tf_op jit(solution)/shard_map/all_to_all | solution.py:67
  221.3 91.8 %reduce-scatter.6.cloned.1.call-start = ((), (), s32[]{:S(2)}) async-start(), calls=%async_computation.7 | async-start | bytes 147456 | tf_op jit(solution)/shard_map/reduce_scatter | solution.py:53
  255.1 0.6 copy-start.2
  365.8 22.8 %copy-start.6 = (s32[8]{0:T(128)S(1)}, s32[8]{0:T(128)}, u32[]{:S(2)}) copy-start(s32[8]{0:T(128)} %get-tuple-element.644) | copy-start | bytes 100
  365.8 22.6 %all-to-all-start.2 = ((bf16[8,8,16,256]{3,2,0,1:T(8,128)(2,1)}), bf16[8,8,16,256]{3,2,0,1:T(8,128)(2,1)S(1)}, u32[]{:S(2)}, u32[]{:S(2)}) async-start(bf16[8,8,16,256]{3,2,0,1:T(8,128)(2,1)} %copy.15), calls=%async_computation.4 | async-start | bytes 1048576 | tf_op jit(solution)/shard_map/all_to_all | solution.py:67
  370.4 83.3 %reduce-scatter.8.cloned.1.call-start = ((), (), s32[]{:S(2)}) async-start(), calls=%async_computation.8 | async-start | bytes 147456 | tf_op jit(solution)/shard_map/reduce_scatter | solution.py:53
  401.1 0.6 copy-start
Sparse Core Ops, SparseCore 0:
  112.8 51.1 reduce-scatter.3
  255.9 57.1 reduce-scatter.5
  401.9 51.7 reduce-scatter.7
where the time goes:
time: 464 us; the launch traced here: 462 us
  waiting for transfers between devices  210 us (45%)
  blocking collectives  158 us (34%)
  loops' own time  34.9 us (8%)
  local copies, waits for them, and re-layouts  16.9 us (4%)
  starting transfers between devices  16.4 us (4%)
  between operations  13.3 us (3%)
  matrix products  12.3 us (3%)
    reduce_scatter x3, waiting for transfers between devices, shards(): lax.psum_scatter(partials[level_index], 'cols', scatter_dimension=0, tile...  161 us
    all_gather x3, blocking collectives, shards(): lax.all_gather(own_solution.astype(jnp.bfloat16)[None], 'rows', axis=0, t...  158 us
    all_to_all x3, waiting for transfers between devices, shards(): lax.all_to_all(grouped, 'cols', split_axis=1, concat_axis=2, tiled=True)  49.2 us
    another operation x3, loops' own time, slot_sum(): return lax.fori_loop(0, live_count, add_block, running)  34.9 us
    all_to_all x3, starting transfers between devices, shards(): lax.all_to_all(grouped, 'cols', split_axis=1, concat_axis=2, tiled=True)  16.3 us
  transfers between devices with their start and end apart: 6, of which 6 were waited for; matrix products, arithmetic and copies ran while one was open for 1% of the time, Pallas kernels for 0%

commit v1 on v0

--- a/solution.py
+++ b/solution.py
@@ -2,6 +2,23 @@
 import jax.numpy as jnp
 from jax import lax
 from jax.sharding import PartitionSpec as P
+
+
+def rest_strips_all_over_axis(q_in):
+    along_axis = "cols"
+    wide_out, response = (lax.psum(1, along_axis), lax.axis_index(along_axis))
+    next_value = list(q_in.shape)
+    g_now = q_in.shape[1] // wide_out
+    next_value[1] = g_now
+    w_next = next_value[2]
+    next_value[2] = w_next * wide_out
+    n_now = jnp.zeros(next_value, q_in.dtype)
+    for no in range(wide_out):
+        opened = lax.dynamic_slice_in_dim(q_in, (response ^ no) * g_now, g_now, axis=1)
+        if no:
+            opened = lax.ppermute(opened, along_axis, [(ii, ii ^ no) for ii in range(wide_out)])
+        n_now = lax.dynamic_update_slice_in_dim(n_now, opened, (response ^ no) * w_next, axis=2)
+    return n_now
 
 
 def locate(source, row_count, col_count):
@@ -64,7 +81,7 @@
                 own_solution.astype(jnp.bfloat16)[None], "rows", axis=0, tiled=True
             )
             grouped = pieces.reshape(per_level, col_count, share_rows, block_width)
-            regrouped = lax.all_to_all(grouped, "cols", split_axis=1, concat_axis=2, tiled=True)
+            regrouped = rest_strips_all_over_axis(grouped)
             solved_store = solved_store.at[
                 level_index * per_level : (level_index + 1) * per_level
             ].set(regrouped[:, 0])

time: 464 us -> 508 us (1.095)
  starting transfers between devices: 16.4 us -> 81.1 us
  waiting for transfers between devices: 210 us -> 186 us
    ppermute x0 -> x21, starting transfers between devices: none -> 81 us  [rest_strips_all_over_axis(): lax.ppermute(opened, along_axis, [(ii, ii ^ no) for ii in range(wide_out)])]
    all_to_all x3 -> x0, waiting for transfers between devices: 49.2 us -> none  [shards(): lax.all_to_all(grouped, 'cols', split_axis=1, concat_axis=2, tiled=True)]
    all_to_all x3 -> x0, starting transfers between devices: 16.3 us -> none  [shards(): lax.all_to_all(grouped, 'cols', split_axis=1, concat_axis=2, tiled=True)]
    ppermute x0 -> x21, waiting for transfers between devices: none -> 13.8 us  [rest_strips_all_over_axis(): lax.ppermute(opened, along_axis, [(ii, ii ^ no) for ii in range(wide_out)])]
    reduce_scatter x3, waiting for transfers between devices: 161 us -> 172 us  [shards(): lax.psum_scatter(partials[level_index], 'cols', scatter_dimension=0, tile...]
    dynamic_slice x10, local copies, waits for them, and re-layouts: 6.43 us -> 11.9 us  [add_block(): source = chosen_ids[slot_index]]
  transfers between devices with their start and end apart: 6 -> 24, of which waited for: 6 -> 7; matrix products, arithmetic and copies ran while one was open for 1% -> 1% of each run, Pallas kernels for 0% -> 0%
where the time goes in v1:
time: 508 us; the launch traced here: 505 us
  waiting for transfers between devices  186 us (37%)
  blocking collectives  158 us (31%)
  starting transfers between devices  81.1 us (16%)
  loops' own time  31.9 us (6%)
  local copies, waits for them, and re-layouts  21.2 us (4%)
  between operations  13.8 us (3%)
  matrix products  12.9 us (3%)
    reduce_scatter x3, waiting for transfers between devices, shards(): lax.psum_scatter(partials[level_index], 'cols', scatter_dimension=0, tile...  172 us
    all_gather x3, blocking collectives, shards(): lax.all_gather(own_solution.astype(jnp.bfloat16)[None], 'rows', axis=0, t...  158 us
    ppermute x21, starting transfers between devices, rest_strips_all_over_axis(): lax.ppermute(opened, along_axis, [(ii, ii ^ no) for ii in range(wide_out)])  81 us
    another operation x3, loops' own time, slot_sum(): return lax.fori_loop(0, live_count, add_block, running)  31.9 us
    ppermute x21, waiting for transfers between devices, rest_strips_all_over_axis(): lax.ppermute(opened, along_axis, [(ii, ii ^ no) for ii in range(wide_out)])  13.8 us
    dynamic_slice x10, local copies, waits for them, and re-layouts, add_block(): source = chosen_ids[slot_index]  11.9 us
  transfers between devices with their start and end apart: 24, of which 7 were waited for; matrix products, arithmetic and copies ran while one was open for 1% of the time, Pallas kernels for 0%

profile of v1, /device:TPU:2, one launch (start us, length us, event | category | flops | bytes accessed | tf_op | source)
XLA Modules:
  0.0 505.3 jit_solution(14049875680792820309)
XLA Ops:
  8.5 56.0 %all-gather = bf16[1024,256]{1,0:T(8,128)(2,1)S(1)} all-gather(bf16[16,256]{1,0:T(8,128)(2,1)S(1)} %get-tuple-element.446), channel_id=2, replica_groups=mesh['rows'=64,'cols'=8] {'rows'}, dimensions={0}, use_global_device_ids=true | all-gather | bytes 532480 | tf_op jit(solution)/shard_map/all_gather | solution.py:80
  64.5 3.5 collective-permute-start
  68.0 4.5 collective-permute-start.1
  72.5 2.1 collective-permute-start.2
  74.7 7.7 %collective-permute-start.3 = (bf16[8,1,16,256]{3,2,0,1:T(8,128)(2,1)S(1)}, bf16[8,1,16,256]{3,2,0,1:T(8,128)(2,1)S(1)}, u32[]{:S(2)}, u32[]{:S(2)}) collective-permute-start(bf16[8,1,16,256]{3,2,0,1:T(8,128)(2,1)S(1)} %get-tuple-element.436), channel_id=1, source_target_pairs={{0,4},{1,5},{2,6},{3,7},{4,0},{5,1},{6,2},{7,3},{8,12},{9,13},{10,... | collective-permute-start | bytes 196616 | tf_op jit(solution)/shard_map/ppermute | solution.py:19
  84.4 3.5 slice_bitcast_fusion
  89.2 5.5 %collective-permute-start.5 = (bf16[8,1,16,256]{3,2,0,1:T(8,128)(2,1)S(1)}, bf16[8,1,16,256]{3,2,0,1:T(8,128)(2,1)S(1)}, u32[]{:S(2)}, u32[]{:S(2)}) collective-permute-start(bf16[8,1,16,256]{3,2,0,1:T(8,128)(2,1)S(1)} %get-tuple-element.434), channel_id=1, source_target_pairs={{0,6},{1,7},{2,4},{3,5},{4,2},{5,3},{6,0},{7,1},{8,14},{9,15},{10,... | collective-permute-start | bytes 196616 | tf_op jit(solution)/shard_map/ppermute | solution.py:19
  98.5 3.6 collective-permute-done.6
  102.3 21.6 %while.42 = (s32[]{:T(128)}, f32[128,256]{1,0:T(8,128)S(1)}, s32[]{:T(128)}, s32[8]{0:T(128)}, bf16[24,128,256]{2,1,0:T(8,128)(2,1)S(1)}, /*index=5*/bf16[8,256,...) while((s32[]{:T(128)}, f32[128,256]{1,0:T(8,128)S(1)}, ...), condition=%wide.region_1.2_spmd, body=%wide.region_0.0_spmd.sunk | while | flops 16810028 | bytes 459350 | solution.py:40
  125.7 53.5 %reduce-scatter.4.cloned.1.call-done = f32[16,256]{1,0:T(8,128)} async-done(((f32[128,256]{1,0:T(8,128)}), f32[16,256]{1,0:T(8,128)}) %reduce-scatter.4.cloned.1.call-update) | async-done | bytes 16400 | tf_op jit(solution)/shard_map/reduce_scatter | solution.py:70
  180.7 50.9 %all-gather.1 = bf16[1024,256]{1,0:T(8,128)(2,1)S(1)} all-gather(bf16[16,256]{1,0:T(8,128)(2,1)S(1)} %get-tuple-element.448), channel_id=3, replica_groups=mesh['rows'=64,'cols'=8] {'rows'}, dimensions={0}, use_global_device_ids=true | all-gather | bytes 532480 | tf_op jit(solution)/shard_map/all_gather | solution.py:80
  231.6 3.0 collective-permute-start.7
  234.6 4.6 collective-permute-start.8
  239.2 2.5 collective-permute-start.9
  241.7 5.2 %collective-permute-start.10 = (bf16[8,1,16,256]{3,2,0,1:T(8,128)(2,1)S(1)}, bf16[8,1,16,256]{3,2,0,1:T(8,128)(2,1)S(1)}, u32[]{:S(2)}, u32[]{:S(2)}) collective-permute-start(bf16[8,1,16,256]{3,2,0,1:T(8,128)(2,1)S(1)} %get-tuple-element.429), channel_id=1, source_target_pairs={{0,4},{1,5},{2,6},{3,7},{4,0},{5,1},{6,2},{7,3},{8,12},{9,13},{10,... | collective-permute-start | bytes 196616 | tf_op jit(solution)/shard_map/ppermute | solution.py:19
  246.9 3.3 collective-permute-start.11
  250.3 4.6 collective-permute-start.12
  255.0 3.7 collective-permute-start.13
  258.8 4.2 collective-permute-done.13
  263.1 15.7 %while.43 = (s32[]{:T(128)}, f32[128,256]{1,0:T(8,128)S(1)}, s32[]{:T(128)}, s32[8]{0:T(128)}, bf16[24,128,256]{2,1,0:T(8,128)(2,1)S(1)}, /*index=5*/bf16[8,256,...) while((s32[]{:T(128)}, f32[128,256]{1,0:T(8,128)S(1)}, ...), condition=%wide.region_4.5_spmd, body=%wide.region_3.4_spmd.sunk | while | flops 16810028 | bytes 459350 | solution.py:40
  279.5 60.2 %reduce-scatter.6.cloned.1.call-done = f32[16,256]{1,0:T(8,128)} async-done(((f32[128,256]{1,0:T(8,128)}), f32[16,256]{1,0:T(8,128)}) %reduce-scatter.6.cloned.1.call-update) | async-done | bytes 16400 | tf_op jit(solution)/shard_map/reduce_scatter | solution.py:70
  341.2 50.9 %all-gather.2 = bf16[1024,256]{1,0:T(8,128)(2,1)S(1)} all-gather(bf16[16,256]{1,0:T(8,128)(2,1)S(1)} %get-tuple-element.450), channel_id=4, replica_groups=mesh['rows'=64,'cols'=8] {'rows'}, dimensions={0}, use_global_device_ids=true | all-gather | bytes 532480 | tf_op jit(solution)/shard_map/all_gather | solution.py:80
  392.2 3.0 collective-permute-start.14
  395.2 4.6 collective-permute-start.15
  399.8 2.5 collective-permute-start.16
  402.3 5.2 %collective-permute-start.17 = (bf16[8,1,16,256]{3,2,0,1:T(8,128)(2,1)S(1)}, bf16[8,1,16,256]{3,2,0,1:T(8,128)(2,1)S(1)}, u32[]{:S(2)}, u32[]{:S(2)}) collective-permute-start(bf16[8,1,16,256]{3,2,0,1:T(8,128)(2,1)S(1)} %get-tuple-element.422), channel_id=1, source_target_pairs={{0,4},{1,5},{2,6},{3,7},{4,0},{5,1},{6,2},{7,3},{8,12},{9,13},{10,... | collective-permute-start | bytes 196616 | tf_op jit(solution)/shard_map/ppermute | solution.py:19
  407.5 3.3 collective-permute-start.18
  410.9 4.6 collective-permute-start.19
  415.6 3.7 collective-permute-start.20
  419.4 4.2 collective-permute-done.20
  423.7 14.6 %while.44 = (s32[]{:T(128)}, f32[128,256]{1,0:T(8,128)S(1)}, s32[]{:T(128)}, s32[8]{0:T(128)}, bf16[24,128,256]{2,1,0:T(8,128)(2,1)S(1)}, /*index=5*/bf16[8,256,...) while((s32[]{:T(128)}, f32[128,256]{1,0:T(8,128)S(1)}, ...), condition=%wide.region_7.8_spmd, body=%wide.region_6.7_spmd.sunk | while | flops 16810028 | bytes 459350 | solution.py:40
  439.0 58.2 %reduce-scatter.8.cloned.1.call-done = f32[16,256]{1,0:T(8,128)} async-done(((f32[128,256]{1,0:T(8,128)}), f32[16,256]{1,0:T(8,128)}) %reduce-scatter.8.cloned.1.call-update) | async-done | bytes 16400 | tf_op jit(solution)/shard_map/reduce_scatter | solution.py:70
  (107 shorter events, 37.0 us)
Async XLA Ops:
  6.5 172.7 %reduce-scatter.4.cloned.1.call-start = ((), (), s32[]{:S(2)}) async-start(), calls=%async_computation.3 | async-start | bytes 147456 | tf_op jit(solution)/shard_map/reduce_scatter | solution.py:70
  64.5 24.7 %collective-permute-start = (bf16[8,1,16,256]{3,2,0,1:T(8,128)(2,1)S(1)}, bf16[8,1,16,256]{3,2,0,1:T(8,128)(2,1)S(1)}, u32[]{:S(2)}, u32[]{:S(2)}) collective-permute-start(bf16[8,1,16,256]{3,2,0,1:T(8,128)(2,1)S(1)} %get-tuple-element.439), channel_id=1, source_target_pairs={{0,1},{1,0},{2,3},{3,2},{4,5},{5,4},{6,7},{7,6},{8,9},{9,8},{10,11... | collective-permute-start | bytes 196616 | tf_op jit(solution)/shard_map/ppermute | solution.py:19
  68.0 26.7 %collective-permute-start.1 = (bf16[8,1,16,256]{3,2,0,1:T(8,128)(2,1)S(1)}, bf16[8,1,16,256]{3,2,0,1:T(8,128)(2,1)S(1)}, u32[]{:S(2)}, u32[]{:S(2)}) collective-permute-start(bf16[8,1,16,256]{3,2,0,1:T(8,128)(2,1)S(1)} %get-tuple-element.438), channel_id=1, source_target_pairs={{0,2},{1,3},{2,0},{3,1},{4,6},{5,7},{6,4},{7,5},{8,10},{9,11},{10,... | collective-permute-start | bytes 196616 | tf_op jit(solution)/shard_map/ppermute | solution.py:19
  72.5 24.1 %collective-permute-start.2 = (bf16[8,1,16,256]{3,2,0,1:T(8,128)(2,1)S(1)}, bf16[8,1,16,256]{3,2,0,1:T(8,128)(2,1)S(1)}, u32[]{:S(2)}, u32[]{:S(2)}) collective-permute-start(bf16[8,1,16,256]{3,2,0,1:T(8,128)(2,1)S(1)} %get-tuple-element.437), channel_id=1, source_target_pairs={{0,3},{1,2},{2,1},{3,0},{4,7},{5,6},{6,5},{7,4},{8,11},{9,10},{10,... | collective-permute-start | bytes 196616 | tf_op jit(solution)/shard_map/ppermute | solution.py:19
  74.7 22.0 %collective-permute-start.3 = (bf16[8,1,16,256]{3,2,0,1:T(8,128)(2,1)S(1)}, bf16[8,1,16,256]{3,2,0,1:T(8,128)(2,1)S(1)}, u32[]{:S(2)}, u32[]{:S(2)}) collective-permute-start(bf16[8,1,16,256]{3,2,0,1:T(8,128)(2,1)S(1)} %get-tuple-element.436), channel_id=1, source_target_pairs={{0,4},{1,5},{2,6},{3,7},{4,0},{5,1},{6,2},{7,3},{8,12},{9,13},{10,... | collective-permute-start | bytes 196616 | tf_op jit(solution)/shard_map/ppermute | solution.py:19
  82.4 14.3 %collective-permute-start.4 = (bf16[8,1,16,256]{3,2,0,1:T(8,128)(2,1)S(1)}, bf16[8,1,16,256]{3,2,0,1:T(8,128)(2,1)S(1)}, u32[]{:S(2)}, u32[]{:S(2)}) collective-permute-start(bf16[8,1,16,256]{3,2,0,1:T(8,128)(2,1)S(1)} %get-tuple-element.435), channel_id=1, source_target_pairs={{0,5},{1,4},{2,7},{3,6},{4,1},{5,0},{6,3},{7,2},{8,13},{9,12},{10,... | collective-permute-start | bytes 196616 | tf_op jit(solution)/shard_map/ppermute | solution.py:19
  84.4 3.6 copy-start.7
  84.4 4.2 copy-start.6
  89.2 9.3 %collective-permute-start.5 = (bf16[8,1,16,256]{3,2,0,1:T(8,128)(2,1)S(1)}, bf16[8,1,16,256]{3,2,0,1:T(8,128)(2,1)S(1)}, u32[]{:S(2)}, u32[]{:S(2)}) collective-permute-start(bf16[8,1,16,256]{3,2,0,1:T(8,128)(2,1)S(1)} %get-tuple-element.434), channel_id=1, source_target_pairs={{0,6},{1,7},{2,4},{3,5},{4,2},{5,3},{6,0},{7,1},{8,14},{9,15},{10,... | collective-permute-start | bytes 196616 | tf_op jit(solution)/shard_map/ppermute | solution.py:19
  94.7 7.4 %collective-permute-start.6 = (bf16[8,1,16,256]{3,2,0,1:T(8,128)(2,1)S(1)}, bf16[8,1,16,256]{3,2,0,1:T(8,128)(2,1)S(1)}, u32[]{:S(2)}, u32[]{:S(2)}) collective-permute-start(bf16[8,1,16,256]{3,2,0,1:T(8,128)(2,1)S(1)} %get-tuple-element.433), channel_id=1, source_target_pairs={{0,7},{1,6},{2,5},{3,4},{4,3},{5,2},{6,1},{7,0},{8,15},{9,14},{10,... | collective-permute-start | bytes 196616 | tf_op jit(solution)/shard_map/ppermute | solution.py:19
  102.3 77.0 %copy-start.3 = (bf16[4,1,256,256]{3,2,1,0:T(8,128)(2,1)S(1)}, bf16[4,1,256,256]{3,2,1,0:T(8,128)(2,1)}, u32[]{:S(2)}) copy-start(bf16[4,1,256,256]{3,2,1,0:T(8,128)(2,1)} %param.19) | copy-start | bytes 1572868
  123.9 0.7 copy-start.1
  124.6 215.2 %reduce-scatter.6.cloned.1.call-start = ((), (), s32[]{:S(2)}) async-start(), calls=%async_computation.4 | async-start | bytes 147456 | tf_op jit(solution)/shard_map/reduce_scatter | solution.py:70
  231.6 18.7 %collective-permute-start.7 = (bf16[8,1,16,256]{3,2,0,1:T(8,128)(2,1)S(1)}, bf16[8,1,16,256]{3,2,0,1:T(8,128)(2,1)S(1)}, u32[]{:S(2)}, u32[]{:S(2)}) collective-permute-start(bf16[8,1,16,256]{3,2,0,1:T(8,128)(2,1)S(1)} %get-tuple-element.432), channel_id=1, source_target_pairs={{0,1},{1,0},{2,3},{3,2},{4,5},{5,4},{6,7},{7,6},{8,9},{9,8},{10,11... | collective-permute-start | bytes 196616 | tf_op jit(solution)/shard_map/ppermute | solution.py:19
  234.6 20.3 %collective-permute-start.8 = (bf16[8,1,16,256]{3,2,0,1:T(8,128)(2,1)S(1)}, bf16[8,1,16,256]{3,2,0,1:T(8,128)(2,1)S(1)}, u32[]{:S(2)}, u32[]{:S(2)}) collective-permute-start(bf16[8,1,16,256]{3,2,0,1:T(8,128)(2,1)S(1)} %get-tuple-element.431), channel_id=1, source_target_pairs={{0,2},{1,3},{2,0},{3,1},{4,6},{5,7},{6,4},{7,5},{8,10},{9,11},{10,... | collective-permute-start | bytes 196616 | tf_op jit(solution)/shard_map/ppermute | solution.py:19
  239.2 19.5 %collective-permute-start.9 = (bf16[8,1,16,256]{3,2,0,1:T(8,128)(2,1)S(1)}, bf16[8,1,16,256]{3,2,0,1:T(8,128)(2,1)S(1)}, u32[]{:S(2)}, u32[]{:S(2)}) collective-permute-start(bf16[8,1,16,256]{3,2,0,1:T(8,128)(2,1)S(1)} %get-tuple-element.430), channel_id=1, source_target_pairs={{0,3},{1,2},{2,1},{3,0},{4,7},{5,6},{6,5},{7,4},{8,11},{9,10},{10,... | collective-permute-start | bytes 196616 | tf_op jit(solution)/shard_map/ppermute | solution.py:19
  241.7 17.0 %collective-permute-start.10 = (bf16[8,1,16,256]{3,2,0,1:T(8,128)(2,1)S(1)}, bf16[8,1,16,256]{3,2,0,1:T(8,128)(2,1)S(1)}, u32[]{:S(2)}, u32[]{:S(2)}) collective-permute-start(bf16[8,1,16,256]{3,2,0,1:T(8,128)(2,1)S(1)} %get-tuple-element.429), channel_id=1, source_target_pairs={{0,4},{1,5},{2,6},{3,7},{4,0},{5,1},{6,2},{7,3},{8,12},{9,13},{10,... | collective-permute-start | bytes 196616 | tf_op jit(solution)/shard_map/ppermute | solution.py:19
  246.9 11.9 %collective-permute-start.11 = (bf16[8,1,16,256]{3,2,0,1:T(8,128)(2,1)S(1)}, bf16[8,1,16,256]{3,2,0,1:T(8,128)(2,1)S(1)}, u32[]{:S(2)}, u32[]{:S(2)}) collective-permute-start(bf16[8,1,16,256]{3,2,0,1:T(8,128)(2,1)S(1)} %get-tuple-element.428), channel_id=1, source_target_pairs={{0,5},{1,4},{2,7},{3,6},{4,1},{5,0},{6,3},{7,2},{8,13},{9,12},{10,... | collective-permute-start | bytes 196616 | tf_op jit(solution)/shard_map/ppermute | solution.py:19
  250.3 8.5 %collective-permute-start.12 = (bf16[8,1,16,256]{3,2,0,1:T(8,128)(2,1)S(1)}, bf16[8,1,16,256]{3,2,0,1:T(8,128)(2,1)S(1)}, u32[]{:S(2)}, u32[]{:S(2)}) collective-permute-start(bf16[8,1,16,256]{3,2,0,1:T(8,128)(2,1)S(1)} %get-tuple-element.427), channel_id=1, source_target_pairs={{0,6},{1,7},{2,4},{3,5},{4,2},{5,3},{6,0},{7,1},{8,14},{9,15},{10,... | collective-permute-start | bytes 196616 | tf_op jit(solution)/shard_map/ppermute | solution.py:19
  255.0 8.1 %collective-permute-start.13 = (bf16[8,1,16,256]{3,2,0,1:T(8,128)(2,1)S(1)}, bf16[8,1,16,256]{3,2,0,1:T(8,128)(2,1)S(1)}, u32[]{:S(2)}, u32[]{:S(2)}) collective-permute-start(bf16[8,1,16,256]{3,2,0,1:T(8,128)(2,1)S(1)} %get-tuple-element.426), channel_id=1, source_target_pairs={{0,7},{1,6},{2,5},{3,4},{4,3},{5,2},{6,1},{7,0},{8,15},{9,14},{10,... | collective-permute-start | bytes 196616 | tf_op jit(solution)/shard_map/ppermute | solution.py:19
  278.8 0.6 copy-start.2
  279.5 217.7 %reduce-scatter.8.cloned.1.call-start = ((), (), s32[]{:S(2)}) async-start(), calls=%async_computation.5 | async-start | bytes 147456 | tf_op jit(solution)/shard_map/reduce_scatter | solution.py:70
  392.2 18.7 %collective-permute-start.14 = (bf16[8,1,16,256]{3,2,0,1:T(8,128)(2,1)S(1)}, bf16[8,1,16,256]{3,2,0,1:T(8,128)(2,1)S(1)}, u32[]{:S(2)}, u32[]{:S(2)}) collective-permute-start(bf16[8,1,16,256]{3,2,0,1:T(8,128)(2,1)S(1)} %get-tuple-element.425), channel_id=1, source_target_pairs={{0,1},{1,0},{2,3},{3,2},{4,5},{5,4},{6,7},{7,6},{8,9},{9,8},{10,11... | collective-permute-start | bytes 196616 | tf_op jit(solution)/shard_map/ppermute | solution.py:19
  395.2 20.3 %collective-permute-start.15 = (bf16[8,1,16,256]{3,2,0,1:T(8,128)(2,1)S(1)}, bf16[8,1,16,256]{3,2,0,1:T(8,128)(2,1)S(1)}, u32[]{:S(2)}, u32[]{:S(2)}) collective-permute-start(bf16[8,1,16,256]{3,2,0,1:T(8,128)(2,1)S(1)} %get-tuple-element.424), channel_id=1, source_target_pairs={{0,2},{1,3},{2,0},{3,1},{4,6},{5,7},{6,4},{7,5},{8,10},{9,11},{10,... | collective-permute-start | bytes 196616 | tf_op jit(solution)/shard_map/ppermute | solution.py:19
  399.8 19.5 %collective-permute-start.16 = (bf16[8,1,16,256]{3,2,0,1:T(8,128)(2,1)S(1)}, bf16[8,1,16,256]{3,2,0,1:T(8,128)(2,1)S(1)}, u32[]{:S(2)}, u32[]{:S(2)}) collective-permute-start(bf16[8,1,16,256]{3,2,0,1:T(8,128)(2,1)S(1)} %get-tuple-element.423), channel_id=1, source_target_pairs={{0,3},{1,2},{2,1},{3,0},{4,7},{5,6},{6,5},{7,4},{8,11},{9,10},{10,... | collective-permute-start | bytes 196616 | tf_op jit(solution)/shard_map/ppermute | solution.py:19
  402.3 17.0 %collective-permute-start.17 = (bf16[8,1,16,256]{3,2,0,1:T(8,128)(2,1)S(1)}, bf16[8,1,16,256]{3,2,0,1:T(8,128)(2,1)S(1)}, u32[]{:S(2)}, u32[]{:S(2)}) collective-permute-start(bf16[8,1,16,256]{3,2,0,1:T(8,128)(2,1)S(1)} %get-tuple-element.422), channel_id=1, source_target_pairs={{0,4},{1,5},{2,6},{3,7},{4,0},{5,1},{6,2},{7,3},{8,12},{9,13},{10,... | collective-permute-start | bytes 196616 | tf_op jit(solution)/shard_map/ppermute | solution.py:19
  407.5 11.8 %collective-permute-start.18 = (bf16[8,1,16,256]{3,2,0,1:T(8,128)(2,1)S(1)}, bf16[8,1,16,256]{3,2,0,1:T(8,128)(2,1)S(1)}, u32[]{:S(2)}, u32[]{:S(2)}) collective-permute-start(bf16[8,1,16,256]{3,2,0,1:T(8,128)(2,1)S(1)} %get-tuple-element.421), channel_id=1, source_target_pairs={{0,5},{1,4},{2,7},{3,6},{4,1},{5,0},{6,3},{7,2},{8,13},{9,12},{10,... | collective-permute-start | bytes 196616 | tf_op jit(solution)/shard_map/ppermute | solution.py:19
  410.9 8.5 %collective-permute-start.19 = (bf16[8,1,16,256]{3,2,0,1:T(8,128)(2,1)S(1)}, bf16[8,1,16,256]{3,2,0,1:T(8,128)(2,1)S(1)}, u32[]{:S(2)}, u32[]{:S(2)}) collective-permute-start(bf16[8,1,16,256]{3,2,0,1:T(8,128)(2,1)S(1)} %get-tuple-element.420), channel_id=1, source_target_pairs={{0,6},{1,7},{2,4},{3,5},{4,2},{5,3},{6,0},{7,1},{8,14},{9,15},{10,... | collective-permute-start | bytes 196616 | tf_op jit(solution)/shard_map/ppermute | solution.py:19
  415.6 8.1 %collective-permute-start.20 = (bf16[8,1,16,256]{3,2,0,1:T(8,128)(2,1)S(1)}, bf16[8,1,16,256]{3,2,0,1:T(8,128)(2,1)S(1)}, u32[]{:S(2)}, u32[]{:S(2)}) collective-permute-start(bf16[8,1,16,256]{3,2,0,1:T(8,128)(2,1)S(1)} %get-tuple-element.419), channel_id=1, source_target_pairs={{0,7},{1,6},{2,5},{3,4},{4,3},{5,2},{6,1},{7,0},{8,15},{9,14},{10,... | collective-permute-start | bytes 196616 | tf_op jit(solution)/shard_map/ppermute | solution.py:19
  423.7 74.4 %copy-start.4 = (f32[16,256]{1,0:T(8,128)S(1)}, f32[16,256]{1,0:T(8,128)}, u32[]{:S(2)}) copy-start(f32[16,256]{1,0:T(8,128)} %get-tuple-element.449) | copy-start | bytes 49156
  423.7 74.4 %copy-start.5 = (f32[16,256]{1,0:T(8,128)S(1)}, f32[16,256]{1,0:T(8,128)}, u32[]{:S(2)}) copy-start(f32[16,256]{1,0:T(8,128)} %get-tuple-element.451) | copy-start | bytes 49156
  438.3 0.6 copy-start
Sparse Core Ops, SparseCore 0:
  124.7 54.4 reduce-scatter.3
  279.6 60.0 reduce-scatter.5
  439.1 58.0 reduce-scatter.7
